TPU v7x, 128 devices: a whole 4x4x4 slice. The times are simulated.
128 devices in a mesh: seq: 16 (over x, z_hi, core), chan: 8 (over y, z_lo).
Axes of the slice: x: 4, y: 4, z: 4 (z_hi: 2, z_lo: 2; z = z_hi * 2 + z_lo), core: 2. Of those that a mesh axis runs over, the one named last changes fastest.
Arguments:
- hidden: bfloat16 [8192, 4096], P('seq', 'chan'), may hold values from -6 to 6
- norm_gain: float32 [2048], replicated, may hold values from 0.25 to 1.75
- w_values: bfloat16 [2048, 4096], P(None, 'chan'), may hold values from -0.125 to 0.125
- w_gates: bfloat16 [2048, 4096], P(None, 'chan'), may hold values from -0.125 to 0.125
- w_control: bfloat16 [2048, 320], replicated, may hold values from -0.046875 to 0.046875
- dt_bias: float32 [64], replicated, may hold values from -1 to 1
- decay_total: float32 [64], replicated, may hold values from 0 to 274
- skip_gain: float32 [64], replicated, may hold values from 0.5 to 2
- gate_gain: float32 [4096], P('chan'), may hold values from 0.25 to 1.75
- w_out: bfloat16 [4096, 2048], P('chan'), may hold values from -0.125 to 0.125
- doc_starts: int32 [4], replicated, may hold values from 0 to 6656, as said below
Outputs:
- layer_out: bfloat16 [8192, 4096], P('seq', 'chan')
Inputs may be any that keep to these rules, and one draw needn't show every extreme that they name: doc_starts[0] is 0 and the offsets rise strictly; document k runs from doc_starts[k] up to the next offset or the window's end.
All inputs are finite; a program needn't handle non-finite values.
Results may differ from a plain program's by a relative error of at most 0.013.
Values may be sent and summed in bfloat16 or wider, within the bound.
A program may use at most 128 MiB of HBM per device.

v0:
```python
import jax
import jax.numpy as jnp
from jax import lax
from jax.experimental import pallas as pl
from jax.experimental.pallas import tpu as pltpu
from jax.sharding import PartitionSpec as P

MESH = pl.DeviceIdType.MESH
F32 = jnp.float32
BF16 = jnp.bfloat16
HIGHEST = lax.Precision.HIGHEST

HEAD_DIM = 64
STATE = 128
CHUNK = 128
ROWS = 512
COLS = 512
HALF = 2048
HEADS = 64
NCHAN = 8
NSEQ = 16
CHUNKS = ROWS // CHUNK
PAIRS = COLS // 128
BLOCK_HEADS = COLS // HEAD_DIM
GROUP = STATE // NSEQ
HALF_ROWS = ROWS // 2
CTRL = 2 * STATE + HEADS
LOG2E = 1.4426950408889634
norm_eps = 1e-05


def dot(a, b):
    return jnp.dot(a, b, preferred_element_type=F32)


def dot_nt(a, b):
    return lax.dot_general(a, b, (((1,), (1,)), ((), ())), preferred_element_type=F32)


def dot_tn(a, b):
    return lax.dot_general(a, b, (((0,), (0,)), ((), ())), preferred_element_type=F32)


def exact(rows, table):
    return jnp.dot(rows, table, precision=HIGHEST, preferred_element_type=F32)


def iota(shape, dim):
    return lax.broadcasted_iota(jnp.int32, shape, dim)


def remote(src, dst, send_sem, recv_sem, device):
    return pltpu.make_async_remote_copy(
        src_ref=src,
        dst_ref=dst,
        send_sem=send_sem,
        recv_sem=recv_sem,
        device_id=device,
        device_id_type=MESH,
    )


def kernel(
    x_hbm, gain_ref, wv_hbm, wg_hbm, wc_hbm, bias_ref, decay_ref, skip_ref, ggain_ref, wo_hbm, docs,
    out_ref,
    x_v, wv, wg, wc, wo, gg, gath, xg, sumsq, rinv,
    c_sc, factors, scores_sc, l_sc, e_sc, lt_sc, et_sc, wval, val, act, reach, chunk_state, tot_sc, totx,
    log_recv, keep_x, st_send, st_recv, enter, en_send, en_recv, y_f, y_b,
    ps_buf, ps_mine, comb, part, rs_buf, relay,
    loc_sem, ag_send, ag_recv, w_send, w_recv, s0_send, s0_recv, s1_send, s1_recv, s2_send, s2_recv,
    ps_send, ps_recv, rs_send, rs_recv,
):
    seq = lax.axis_index("seq")
    chan = lax.axis_index("chan")
    yy = chan // 2
    zz = chan % 2
    y_near = yy + 1 - 2 * (yy % 2)
    c_n = y_near * 2 + zz
    c_o = yy * 2 + 1 - zz
    c_d = y_near * 2 + 1 - zz
    c_w = (3 - yy) * 2 + zz
    mirrored = chan >= 4

    def block_of(c):
        return jnp.where(mirrored, 7 - c, c)

    k_me, k_n, k_o, k_d = block_of(chan), block_of(c_n), block_of(c_o), block_of(c_d)
    to_n, to_o, to_d, to_w = {"chan": c_n}, {"chan": c_o}, {"chan": c_d}, {"chan": c_w}
    to_right, to_left = {"seq": (seq + 4) % NSEQ}, {"seq": (seq + 12) % NSEQ}
    to_twin = {"seq": seq + 1 - 2 * (seq % 2)}
    q_me = (seq // 4) * 2 + seq % 2
    q_twin = (seq // 4) * 2 + 1 - seq % 2

    barrier = pltpu.get_barrier_semaphore()
    for device in (to_n, to_o, to_d, to_w):
        pl.semaphore_signal(barrier, inc=1, device_id=device, device_id_type=MESH)

    def greet_seq(k, carry_):
        pl.semaphore_signal(barrier, inc=1, device_id={"seq": (seq + k) % NSEQ}, device_id_type=MESH)
        return carry_

    lax.fori_loop(1, NSEQ, greet_seq, 0)

    x_copy = pltpu.make_async_copy(x_hbm, x_v, loc_sem.at[0])
    x_copy.start()
    v_copy = pltpu.make_async_copy(wv_hbm, wv.at[0], loc_sem.at[1])
    c_copy = pltpu.make_async_copy(wc_hbm, wc, loc_sem.at[2])
    g_copy = pltpu.make_async_copy(wg_hbm, wg.at[0], loc_sem.at[3])
    o_copy = pltpu.make_async_copy(wo_hbm, wo.at[0], loc_sem.at[4])

    col = iota((COLS, COLS), 1)
    wanted = jnp.where(mirrored, COLS - 1 - col, col)
    flip = jnp.where(iota((COLS, COLS), 0) == wanted, 1.0, 0.0).astype(BF16)
    x_copy.wait()
    gath[k_me] = dot(x_v[...], flip).astype(BF16)
    gg[0] = ggain_ref[...]

    pl.semaphore_wait(barrier, 4 + NSEQ - 1)

    h1, h2 = pl.ds(0, HALF_ROWS), pl.ds(HALF_ROWS, HALF_ROWS)
    whole = pl.ds(0, ROWS)
    started = []

    def send(src, dst, send_sem, recv_sem, device):
        copy = remote(src, dst, send_sem, recv_sem, device)
        copy.start()
        started.append(copy)

    def ag(kind, block, rows, device):
        ref = gath.at[block, rows]
        send(ref, ref, ag_send.at[kind], ag_recv.at[kind], device)

    def ag_wait(kind, block, rows):
        ref = gath.at[block, rows]
        remote(ref, ref, ag_send.at[kind], ag_recv.at[kind], to_n).wait_recv()

    tensors = ((wv_hbm, wv, HALF // 8), (wg_hbm, wg, HALF // 8), (wo_hbm, wo, COLS // 8))

    def w_rows(t, dx, twin, half):
        size = tensors[t][2]
        q = ((q_twin if twin else q_me) + 2 * dx) % 8
        if half is None:
            return pl.ds(pl.multiple_of(q * size, size), size)
        return pl.ds(pl.multiple_of(q * size + half * (size // 2), size // 2), size // 2)

    def w_from_partner(t):
        hbm, buf, _ = tensors[t]
        rows = w_rows(t, 0, False, None)
        send(hbm.at[rows], buf.at[1, rows], w_send.at[t, 0], w_recv.at[t, 0], to_w)

    def w_on(t, kind, dx, half, device):
        ref = tensors[t][1].at[1, w_rows(t, dx, False, half)]
        send(ref, ref, w_send.at[t, kind], w_recv.at[t, kind], device)

    def w_wait(t, kind, dx, twin, half):
        ref = tensors[t][1].at[1, w_rows(t, dx, twin, half)]
        remote(ref, ref, w_send.at[t, kind], w_recv.at[t, kind], to_w).wait_recv()

    def w_stage1(t):
        w_wait(t, 0, 0, False, None)
        w_on(t, 1, 0, None, to_right)
        w_on(t, 2, 0, None, to_left)
        w_on(t, 3, 0, None, to_twin)

    def w_stage2(t):
        w_wait(t, 1, 3, False, None)
        w_on(t, 4, 3, 0, to_right)
        w_on(t, 5, 3, None, to_twin)
        w_wait(t, 2, 1, False, None)
        w_on(t, 6, 1, 1, to_left)
        w_on(t, 7, 1, None, to_twin)

    def w_stage3(t):
        w_wait(t, 4, 2, False, 0)
        w_on(t, 8, 2, 0, to_twin)
        w_wait(t, 6, 2, False, 1)
        w_on(t, 9, 2, 1, to_twin)

    def w_finish(t):
        w_wait(t, 3, 0, True, None)
        w_wait(t, 5, 3, True, None)
        w_wait(t, 7, 1, True, None)
        w_wait(t, 8, 2, True, 0)
        w_wait(t, 9, 2, True, 1)

    ag(0, k_me, h1, to_n)
    ag(2, k_me, h2, to_o)
    w_from_partner(0)
    ag(1, k_me, h2, to_n)
    ag(3, k_me, h1, to_o)
    w_from_partner(1)
    send(ggain_ref, gg.at[1], ag_send.at[6], ag_recv.at[6], to_w)
    for copy in (v_copy, c_copy, g_copy, o_copy):
        copy.start()

    def scale_block(k):
        gain = gain_ref[k]
        lanes = pl.ds(pl.multiple_of(k * COLS, COLS), COLS)

        def scale_rows(i, carry_):
            rows = pl.ds(pl.multiple_of(i * 64, 64), 64)
            x = gath[k, rows, :].astype(F32)
            xg[rows, lanes] = (x * gain).astype(BF16)
            sq = x * x
            sumsq[rows, :] += sq[:, 0:128] + sq[:, 128:256] + sq[:, 256:384] + sq[:, 384:512]
            return carry_

        lax.fori_loop(0, ROWS // 64, scale_rows, 0)

    sumsq[...] = jnp.zeros_like(sumsq)
    scale_block(k_me)

    lane = iota((HEADS, 128), 1)
    head = iota((HEADS, 128), 0)
    picked = ((head == chan * BLOCK_HEADS + lane) & (lane < BLOCK_HEADS)) | (
        (head == (c_w - 1) * BLOCK_HEADS + lane) & (lane >= BLOCK_HEADS) & (lane < 2 * BLOCK_HEADS)
    )
    pick = jnp.where(picked, 1.0, 0.0)
    spread = jnp.where(iota((128, 2 * COLS), 0) == iota((128, 2 * COLS), 1) // HEAD_DIM, 1.0, 0.0)
    pick_b = pick.astype(BF16)
    spread_b = spread.astype(BF16)

    def head_row(ref):
        return exact(jnp.broadcast_to(ref[...], (8, HEADS)), pick)

    bias = head_row(bias_ref)[0:1]
    slope = head_row(decay_ref)[0:1] * (-LOG2E / (ROWS * NSEQ))
    skip_x = exact(head_row(skip_ref), spread)[0:1]

    starts = [docs[k] for k in range(4)]
    base = seq * ROWS

    def seg_at(position):
        total = jnp.int32(0)
        for start in starts:
            total = total + jnp.where(position >= start, 1, 0)
        return total

    def same(a, b):
        return jnp.where(seg_at(a) == seg_at(b), 1.0, 0.0)

    def keep_f(begin, end):
        return same(end, begin - 1)

    def keep_b(begin, end):
        return same(begin, end + 1)

    sub = iota((CHUNK, CHUNK), 0)
    lan = iota((CHUNK, CHUNK), 1)
    lower = jnp.where(sub >= lan, 1.0, 0.0).astype(BF16)
    upper = jnp.where(sub <= lan, 1.0, 0.0).astype(BF16)

    ag_wait(0, k_n, h1)
    ag(4, k_n, h1, to_o)
    ag_wait(2, k_o, h2)
    ag(5, k_o, h2, to_n)
    w_stage1(0)
    ag_wait(1, k_n, h2)
    scale_block(k_n)
    ag_wait(3, k_o, h1)
    scale_block(k_o)
    w_stage1(1)
    w_from_partner(2)
    w_stage2(0)
    w_stage3(0)
    ag_wait(4, k_d, h1)
    ag_wait(5, k_d, h2)
    scale_block(k_d)

    for i in range(CHUNKS):
        rows = pl.ds(i * CHUNK, CHUNK)
        total = jnp.sum(sumsq[rows, :], axis=1, keepdims=True)
        rinv[rows, :] = jnp.broadcast_to(lax.rsqrt(total * (1.0 / HALF) + norm_eps), (CHUNK, 128))

    def project_control(i, carry_):
        rows = pl.ds(pl.multiple_of(i * 256, 256), 256)
        c_sc[rows, :] = (dot_nt(xg[rows, :], wc[...]) * rinv[rows, :][:, 0:1]).astype(BF16)
        return carry_

    def project_values(blk):
        def go(i, carry_):
            rows = pl.ds(pl.multiple_of(i * 256, 256), 256)
            val[blk, rows, :] = (dot(xg[rows, :], wv[blk]) * rinv[rows, :][:, 0:1]).astype(BF16)
            return carry_

        lax.fori_loop(0, 2, go, 0)

    def project_gates(blk):
        def go(i, carry_):
            rows = pl.ds(pl.multiple_of(i * 256, 256), 256)
            g = (dot(xg[rows, :], wg[blk]) * rinv[rows, :][:, 0:1]).astype(BF16).astype(F32)
            act[blk, rows, :] = g / (1.0 + jnp.exp(-g))
            return carry_

        lax.fori_loop(0, 2, go, 0)

    c_copy.wait()
    lax.fori_loop(0, 2, project_control, 0)
    v_copy.wait()
    project_values(0)
    w_stage2(1)
    w_stage1(2)

    def compact(c, carry_):
        rows = pl.ds(pl.multiple_of(c * CHUNK, CHUNK), CHUNK)
        begin = base + c * CHUNK
        end = begin + CHUNK - 1
        ctl = c_sc[rows, :]
        z = dot(ctl[:, 2 * STATE :], pick_b) + bias
        step = jnp.maximum(z, 0.0) + jnp.log1p(jnp.exp(-jnp.abs(z)))
        log_rate = slope * step
        p1 = log_rate.astype(BF16)
        rest = log_rate - p1.astype(F32)
        p2 = rest.astype(BF16)
        p3 = (rest - p2.astype(F32)).astype(BF16)
        run = dot(lower, p1) + dot(lower, p2) + dot(lower, p3)
        before = run - log_rate
        total = run[CHUNK - 1 : CHUNK, :]
        l_sc[0, rows, :] = run
        e_sc[0, rows, :] = before
        l_sc[1, rows, :] = pltpu.roll(run, 128 - BLOCK_HEADS, 1)
        e_sc[1, rows, :] = pltpu.roll(before, 128 - BLOCK_HEADS, 1)
        run_t = run.T
        before_t = before.T
        for blk in range(2):
            lt_sc[blk, c] = run_t[blk * BLOCK_HEADS : (blk + 1) * BLOCK_HEADS, :]
            et_sc[blk, c] = before_t[blk * BLOCK_HEADS : (blk + 1) * BLOCK_HEADS, :]
        tot_sc[c] = jnp.broadcast_to(total, (8, 128))
        seg = seg_at(begin + sub)

        def mask(position):
            return jnp.where(seg == seg_at(position), 1.0, 0.0)

        out_f = jnp.exp2(total - run) * mask(end)
        out_b = jnp.exp2(before) * mask(begin)
        in_f = jnp.exp2(run) * mask(begin - 1)
        in_b = jnp.exp2(total - before) * mask(end + 1)
        factors[c] = jnp.concatenate([step, step * out_f, step * out_b, in_f, in_b], axis=0).astype(BF16)
        scores = dot_nt(ctl[:, STATE : 2 * STATE], ctl[:, 0:STATE])
        scores_sc[c] = jnp.where(seg == seg_at(begin + lan), scores, 0.0)
        return carry_

    lax.fori_loop(0, CHUNKS, compact, 0)
    tot_sc[CHUNKS] = tot_sc[0] + tot_sc[1] + tot_sc[2] + tot_sc[3]
    log_recv[seq] = tot_sc[CHUNKS]

    def log_copy(k):
        peer = (seq + k) % NSEQ
        return remote(
            tot_sc.at[CHUNKS], log_recv.at[seq], s0_send.at[k], s0_recv.at[k], {"seq": peer}
        )

    def send_log(k, carry_):
        log_copy(k).start()
        return carry_

    lax.fori_loop(1, NSEQ, send_log, 0)

    def states_of(blk):
        spread_blk = spread_b[:, blk * COLS : (blk + 1) * COLS]

        def states(c, carry_):
            rows = pl.ds(pl.multiple_of(c * CHUNK, CHUNK), CHUNK)
            v = val[blk, rows, :].astype(F32)
            wide = dot(factors[c], spread_blk)
            wval[blk, rows, :] = (wide[0:CHUNK] * v).astype(BF16)
            weighted = jnp.concatenate(
                [wide[CHUNK : 2 * CHUNK] * v, wide[2 * CHUNK : 3 * CHUNK] * v], axis=1
            ).astype(BF16)
            reach[blk, 0, rows, :] = wide[3 * CHUNK : 4 * CHUNK].astype(BF16)
            reach[blk, 1, rows, :] = wide[4 * CHUNK : 5 * CHUNK].astype(BF16)
            chunk_state[blk * CHUNKS + c] = dot_tn(c_sc[rows, 0:STATE], weighted)
            return carry_

        lax.fori_loop(0, CHUNKS, states, 0)

    states_of(0)
    w_stage3(1)
    w_finish(0)
    project_values(1)
    states_of(1)

    spread_of = [spread[:, 0:COLS], spread[:, COLS:]]
    for blk in range(2):
        for c in range(CHUNKS):
            totx[blk, c] = jnp.exp2(exact(tot_sc[c], spread_of[blk]))
        f = chunk_state[blk * CHUNKS, :, 0:COLS]
        for c in range(1, CHUNKS):
            begin = base + c * CHUNK
            f = chunk_state[blk * CHUNKS + c, :, 0:COLS] + (
                totx[blk, c, 0:1, :] * keep_f(begin, begin + CHUNK - 1)
            ) * f
        b = chunk_state[blk * CHUNKS + CHUNKS - 1, :, COLS:]
        for c in range(CHUNKS - 2, -1, -1):
            begin = base + c * CHUNK
            b = chunk_state[blk * CHUNKS + c, :, COLS:] + (
                totx[blk, c, 0:1, :] * keep_b(begin, begin + CHUNK - 1)
            ) * b
        st_send[:, blk] = jnp.concatenate(
            [f.reshape(NSEQ, GROUP, COLS), b.reshape(NSEQ, GROUP, COLS)], axis=1
        ).astype(BF16)

    def state_copy(k):
        peer = (seq + k) % NSEQ
        return remote(
            st_send.at[peer], st_recv.at[seq], s1_send.at[k], s1_recv.at[k], {"seq": peer}
        )

    def send_state(k, carry_):
        state_copy(k).start()
        return carry_

    lax.fori_loop(1, NSEQ, send_state, 0)
    st_recv[seq] = st_send[seq]

    left = iota((CHUNK, 128), 1) < HEAD_DIM

    def within_of(blk):
        def within(c, carry_):
            rows = pl.ds(pl.multiple_of(c * CHUNK, CHUNK), CHUNK)
            scores = scores_sc[c]
            run = l_sc[blk, rows, :]
            before = e_sc[blk, rows, :]
            run_t = lt_sc[blk, c]
            before_t = et_sc[blk, c]
            for pair in range(PAIRS):
                fs, bs = [], []
                for h in (2 * pair, 2 * pair + 1):
                    gap = jnp.minimum(
                        run[:, h : h + 1] - run_t[h : h + 1, :],
                        before_t[h : h + 1, :] - before[:, h : h + 1],
                    )
                    g = (jnp.exp2(gap) * scores).astype(BF16)
                    fs.append(g * lower)
                    bs.append(g * upper)
                lhs = jnp.concatenate(
                    [jnp.concatenate(fs, axis=1), jnp.concatenate(bs, axis=1)], axis=0
                )
                lanes = slice(pair * 128, pair * 128 + 128)
                w = wval[blk, rows, lanes].astype(F32)
                rhs = jnp.concatenate([jnp.where(left, w, 0.0), jnp.where(left, 0.0, w)], axis=0)
                y = dot(lhs, rhs.astype(BF16))
                wide = slice(blk * COLS + pair * 128, blk * COLS + pair * 128 + 128)
                direct = skip_x[:, wide] * val[blk, rows, lanes].astype(F32)
                y_f[blk, rows, lanes] = y[0:CHUNK] + direct
                y_b[blk, rows, lanes] = y[CHUNK:] + direct
            return carry_

        lax.fori_loop(0, CHUNKS, within, 0)

    within_of(0)
    w_stage2(2)

    def await_log(k, carry_):
        src = (seq + NSEQ - k) % NSEQ
        remote(
            tot_sc.at[CHUNKS], log_recv.at[src], s0_send.at[k], s0_recv.at[k], {"seq": src}
        ).wait_recv()
        return carry_

    lax.fori_loop(1, NSEQ, await_log, 0)
    keep_x[...] = jnp.exp2(exact(log_recv[...].reshape(NSEQ * 8, 128), spread)).reshape(NSEQ, 8, 2 * COLS)

    def await_state(k, carry_):
        src = (seq + NSEQ - k) % NSEQ
        remote(
            st_send.at[src], st_recv.at[src], s1_send.at[k], s1_recv.at[k], {"seq": src}
        ).wait_recv()
        return carry_

    lax.fori_loop(1, NSEQ, await_state, 0)

    for blk in range(2):
        lanes = slice(blk * COLS, (blk + 1) * COLS)
        now = jnp.zeros((GROUP, COLS), F32)
        for d in range(NSEQ):
            enter[d, blk] = now
            if d < NSEQ - 1:
                begin = d * ROWS
                kept = keep_x[d, :, lanes] * keep_f(begin, begin + ROWS - 1)
                now = st_recv[d, blk].astype(F32)[0:GROUP] + kept * now
        now = jnp.zeros((GROUP, COLS), F32)
        for d in range(NSEQ - 1, -1, -1):
            en_send[d, blk] = jnp.concatenate([enter[d, blk], now], axis=0).astype(BF16)
            if d > 0:
                begin = d * ROWS
                kept = keep_x[d, :, lanes] * keep_b(begin, begin + ROWS - 1)
                now = st_recv[d, blk].astype(F32)[GROUP : 2 * GROUP] + kept * now

    def enter_copy(k):
        peer = (seq + k) % NSEQ
        return remote(
            en_send.at[peer], en_recv.at[seq], s2_send.at[k], s2_recv.at[k], {"seq": peer}
        )

    def send_enter(k, carry_):
        enter_copy(k).start()
        return carry_

    lax.fori_loop(1, NSEQ, send_enter, 0)
    en_recv[seq] = en_send[seq]
    w_stage3(2)

    within_of(1)

    g_copy.wait()
    project_gates(0)
    w_finish(1)
    project_gates(1)

    def await_enter(k, carry_):
        src = (seq + NSEQ - k) % NSEQ
        remote(
            en_send.at[src], en_recv.at[src], s2_send.at[k], s2_recv.at[k], {"seq": src}
        ).wait_recv()
        return carry_

    lax.fori_loop(1, NSEQ, await_enter, 0)

    for blk in range(2):
        both = en_recv[:, blk].astype(F32)
        f = both[:, 0:GROUP].reshape(STATE, COLS)
        b = both[:, GROUP : 2 * GROUP].reshape(STATE, COLS)
        for c in range(CHUNKS):
            rows = pl.ds(c * CHUNK, CHUNK)
            begin = base + c * CHUNK
            cc = c_sc[rows, STATE : 2 * STATE]
            y_f[blk, rows, :] += dot(cc, f.astype(BF16)) * reach[blk, 0, rows, :].astype(F32)
            if c < CHUNKS - 1:
                f = chunk_state[blk * CHUNKS + c, :, 0:COLS] + (
                    totx[blk, c, 0:1, :] * keep_f(begin, begin + CHUNK - 1)
                ) * f
        for c in range(CHUNKS - 1, -1, -1):
            rows = pl.ds(c * CHUNK, CHUNK)
            begin = base + c * CHUNK
            cc = c_sc[rows, STATE : 2 * STATE]
            y_b[blk, rows, :] += dot(cc, b.astype(BF16)) * reach[blk, 1, rows, :].astype(F32)
            if c > 0:
                b = chunk_state[blk * CHUNKS + c, :, COLS:] + (
                    totx[blk, c, 0:1, :] * keep_b(begin, begin + CHUNK - 1)
                ) * b

    ones = jnp.ones((8, COLS), BF16)
    row8 = iota((8, CHUNK), 0)

    def gate(c, carry_):
        rows = pl.ds(pl.multiple_of(c * CHUNK, CHUNK), CHUNK)
        sums = jnp.zeros((8, CHUNK), F32)
        for blk in range(2):
            a = act[blk, rows, :]
            for d, y in enumerate((y_f, y_b)):
                v = y[blk, rows, :] * a
                y[blk, rows, :] = v
                sq = v * v
                hi = sq.astype(BF16)
                lo = (sq - hi.astype(F32)).astype(BF16)
                sums = sums + jnp.where(row8 == d, dot_nt(ones, hi) + dot_nt(ones, lo), 0.0)
        ps_mine[:, rows] = sums
        return carry_

    lax.fori_loop(0, CHUNKS, gate, 0)
    for k, device in enumerate((to_d, to_n, to_o)):
        send(ps_mine, ps_buf.at[k], ps_send.at[k], ps_recv.at[k], device)
    w_finish(2)
    o_copy.wait()
    remote(ggain_ref, gg.at[1], ag_send.at[6], ag_recv.at[6], to_w).wait_recv()
    for k in range(3):
        remote(ps_mine, ps_buf.at[k], ps_send.at[k], ps_recv.at[k], to_n).wait_recv()
    sums = ps_mine[...] + ps_buf[0] + ps_buf[1] + ps_buf[2]
    scale = lax.rsqrt(sums * (1.0 / (COLS * NCHAN)) + norm_eps)
    scale = jnp.concatenate([scale, jnp.zeros((CHUNK - 8, ROWS), F32)], axis=0)
    for c in range(CHUNKS):
        rinv[c * CHUNK : (c + 1) * CHUNK, :] = scale[:, c * CHUNK : (c + 1) * CHUNK].T

    def combine(c, carry_):
        rows = pl.ds(pl.multiple_of(c * CHUNK, CHUNK), CHUNK)
        r = rinv[rows, :]
        for blk in range(2):
            both = y_f[blk, rows, :] * r[:, 0:1] + y_b[blk, rows, :] * r[:, 1:2]
            comb[rows, blk * COLS : (blk + 1) * COLS] = (both * gg[blk]).astype(BF16)
        return carry_

    lax.fori_loop(0, CHUNKS, combine, 0)

    def out_block(k):
        lanes = pl.ds(pl.multiple_of(k * COLS, COLS), COLS)

        def block(i, carry_):
            rows = pl.ds(pl.multiple_of(i * 256, 256), 256)
            part[k, rows, :] = (
                dot(comb[rows, 0:COLS], wo[0, :, lanes]) + dot(comb[rows, COLS:], wo[1, :, lanes])
            ).astype(BF16)
            return carry_

        lax.fori_loop(0, 2, block, 0)

    def rs(kind, src, dst, device):
        send(src, dst, rs_send.at[kind], rs_recv.at[kind], device)

    def rs_wait(kind, dst):
        remote(part.at[k_me, h1], dst, rs_send.at[kind], rs_recv.at[kind], to_n).wait_recv()

    def add(block, rows, ref):
        part[block, rows, :] = (part[block, rows, :].astype(F32) + ref[...].astype(F32)).astype(BF16)

    out_block(k_d)
    rs(0, part.at[k_d, h1], relay.at[0], to_o)
    rs(1, part.at[k_d, h2], relay.at[1], to_n)

    def out_second(i, carry_):
        out_block(jnp.where(i == 0, k_n, k_o))
        return carry_

    lax.fori_loop(0, 2, out_second, 0)
    rs(2, part.at[k_n, h2], rs_buf.at[0, h2], to_n)
    rs(4, part.at[k_o, h1], rs_buf.at[1, h1], to_o)
    out_block(k_me)
    rs_wait(0, relay.at[0])
    add(k_n, h1, relay.at[0])
    rs(3, part.at[k_n, h1], rs_buf.at[0, h1], to_n)
    rs_wait(1, relay.at[1])
    add(k_o, h2, relay.at[1])
    rs(5, part.at[k_o, h2], rs_buf.at[1, h2], to_o)

    def finish(i, rows):
        total = part[k_me, rows, :].astype(F32) + rs_buf[0, rows, :].astype(F32) + rs_buf[1, rows, :].astype(F32)
        out_ref[rows, :] = dot(total.astype(BF16), flip).astype(BF16)

    rs_wait(4, rs_buf.at[1, h1])
    rs_wait(2, rs_buf.at[0, h2])
    rs_wait(3, rs_buf.at[0, h1])
    finish(0, h1)
    rs_wait(5, rs_buf.at[1, h2])
    finish(1, h2)

    for copy in started:
        copy.wait_send()

    def sent_seq(k, carry_):
        log_copy(k).wait_send()
        state_copy(k).wait_send()
        enter_copy(k).wait_send()
        return carry_

    lax.fori_loop(1, NSEQ, sent_seq, 0)


def local(
    hidden, norm_gain, w_values, w_gates, w_control, dt_bias, decay_total, skip_gain, gate_gain, w_out, doc_starts
):
    vmem = pl.BlockSpec(memory_space=pltpu.VMEM)
    hbm = pl.BlockSpec(memory_space=pl.ANY)
    smem = pl.BlockSpec(memory_space=pltpu.SMEM)
    dma = pltpu.SemaphoreType.DMA
    scratch = [
        pltpu.VMEM((ROWS, COLS), BF16),
        pltpu.VMEM((2, HALF, COLS), BF16),
        pltpu.VMEM((2, HALF, COLS), BF16),
        pltpu.VMEM((CTRL, HALF), BF16),
        pltpu.VMEM((2, COLS, HALF), BF16),
        pltpu.VMEM((2, 1, COLS), F32),
        pltpu.VMEM((4, ROWS, COLS), BF16),
        pltpu.VMEM((ROWS, HALF), BF16),
        pltpu.VMEM((ROWS, 128), F32),
        pltpu.VMEM((ROWS, 128), F32),
        pltpu.VMEM((ROWS, CTRL), BF16),
        pltpu.VMEM((CHUNKS, 5 * CHUNK, 128), BF16),
        pltpu.VMEM((CHUNKS, CHUNK, CHUNK), F32),
        pltpu.VMEM((2, ROWS, 128), F32),
        pltpu.VMEM((2, ROWS, 128), F32),
        pltpu.VMEM((2, CHUNKS, 8, 128), F32),
        pltpu.VMEM((2, CHUNKS, 8, 128), F32),
        pltpu.VMEM((2, ROWS, COLS), BF16),
        pltpu.VMEM((2, ROWS, COLS), BF16),
        pltpu.VMEM((2, ROWS, COLS), F32),
        pltpu.VMEM((2, 2, ROWS, COLS), BF16),
        pltpu.VMEM((2 * CHUNKS, STATE, 2 * COLS), F32),
        pltpu.VMEM((CHUNKS + 1, 8, 128), F32),
        pltpu.VMEM((2, CHUNKS, 8, COLS), F32),
        pltpu.VMEM((NSEQ, 8, 128), F32),
        pltpu.VMEM((NSEQ, 8, 2 * COLS), F32),
        pltpu.VMEM((NSEQ, 2, 2 * GROUP, COLS), BF16),
        pltpu.VMEM((NSEQ, 2, 2 * GROUP, COLS), BF16),
        pltpu.VMEM((NSEQ, 2, GROUP, COLS), F32),
        pltpu.VMEM((NSEQ, 2, 2 * GROUP, COLS), BF16),
        pltpu.VMEM((NSEQ, 2, 2 * GROUP, COLS), BF16),
        pltpu.VMEM((2, ROWS, COLS), F32),
        pltpu.VMEM((2, ROWS, COLS), F32),
        pltpu.VMEM((3, 8, ROWS), F32),
        pltpu.VMEM((8, ROWS), F32),
        pltpu.VMEM((ROWS, 2 * COLS), BF16),
        pltpu.VMEM((4, ROWS, COLS), BF16),
        pltpu.VMEM((2, ROWS, COLS), BF16),
        pltpu.VMEM((2, HALF_ROWS, COLS), BF16),
        dma((5,)),
        dma((7,)),
        dma((7,)),
        dma((3, 10)),
        dma((3, 10)),
        dma((NSEQ,)),
        dma((NSEQ,)),
        dma((NSEQ,)),
        dma((NSEQ,)),
        dma((NSEQ,)),
        dma((NSEQ,)),
        dma((3,)),
        dma((3,)),
        dma((6,)),
        dma((6,)),
    ]
    return pl.pallas_call(
        kernel,
        name="mixer",
        out_shape=jax.ShapeDtypeStruct((ROWS, COLS), BF16),
        in_specs=[hbm, vmem, hbm, hbm, hbm, vmem, vmem, vmem, vmem, hbm, smem],
        out_specs=vmem,
        scratch_shapes=scratch,
        compiler_params=pltpu.CompilerParams(
            collective_id=0, has_side_effects=True, vmem_limit_bytes=56 * 2**20
        ),
    )(
        hidden,
        norm_gain.reshape(4, 1, COLS),
        w_values,
        w_gates,
        w_control.T,
        dt_bias.reshape(1, HEADS),
        decay_total.reshape(1, HEADS),
        skip_gain.reshape(1, HEADS),
        gate_gain.reshape(1, COLS),
        w_out,
        doc_starts,
    )


def solution(mesh):
    in_specs = (
        P("seq", "chan"),
        P(),
        P(None, "chan"),
        P(None, "chan"),
        P(),
        P(),
        P(),
        P(),
        P("chan"),
        P("chan", None),
        P(),
    )
    return jax.shard_map(local, mesh=mesh, in_specs=in_specs, out_specs=P("seq", "chan"), check_vma=False)
```

profile of v0, /device:TPU:0, one launch (start us, length us, event | category | flops | bytes accessed | tf_op | source)
XLA Modules:
  0.0 95.1 jit_solution(17533590530545237484)
XLA Ops:
  0.0 93.2 %mixer.1 = bf16[512,512]{1,0:T(8,128)(2,1)} custom-call(bf16[512,512]{1,0:T(8,128)(2,1)} %x_hbm.1, f32[4,1,512]{2,1,0:T(1,128)} %bitcast.7, bf16[2048,512]{1,0:T(8,128)(2,1)} %wv_hbm.1, bf16[2048,512]{1,0:T(8,128)(2,1)} %wg_hbm.1, bf16[320,2048]{1,0:T(8,128)(2,1)} %bitcast.6, f32[1,64]{1,0:T(1,128)} %bitcast.9, f32[1,64]{1,0:T(1,128)} %bitcast.10, ...), custom_call_target="tpu_custom_call" | custom-call | tf_op jit(solution)/shard_map/mixer/pallas_call | solution.py:711
  93.2 1.9 %copy.13 = bf16[512,512]{1,0:T(8,128)(2,1)} copy(bf16[512,512]{1,0:T(8,128)(2,1)} %mixer.1) | data formatting | bytes 1048576
where the time goes:
time: 95.3 us; the launch traced here: 95.1 us
  Pallas kernels  93.2 us (98%)
  local copies, waits for them, and re-layouts  1.87 us (2%)
    pallas_call x1, Pallas kernels, local(): pl.pallas_call(kernel, name='mixer', out_shape=jax.ShapeDtypeStruct((ROWS...  93.2 us

commit v1 on v0

--- a/solution.py
+++ b/solution.py
@@ -106,7 +106,7 @@
     v_copy = pltpu.make_async_copy(wv_hbm, wv.at[0], loc_sem.at[1])
     c_copy = pltpu.make_async_copy(wc_hbm, wc, loc_sem.at[2])
     g_copy = pltpu.make_async_copy(wg_hbm, wg.at[0], loc_sem.at[3])
-    o_copy = pltpu.make_async_copy(wo_hbm, wo.at[0], loc_sem.at[4])
+    o_copy = pltpu.make_async_copy(wo_hbm, wo.at[pl.ds(0, COLS)], loc_sem.at[4])
 
     col = iota((COLS, COLS), 1)
     wanted = jnp.where(mirrored, COLS - 1 - col, col)
@@ -134,7 +134,7 @@
         ref = gath.at[block, rows]
         remote(ref, ref, ag_send.at[kind], ag_recv.at[kind], to_n).wait_recv()
 
-    tensors = ((wv_hbm, wv, HALF // 8), (wg_hbm, wg, HALF // 8), (wo_hbm, wo, COLS // 8))
+    tensors = ((wv_hbm, wv, HALF // 8), (wg_hbm, wg, HALF // 8))
 
     def w_rows(t, dx, twin, half):
         size = tensors[t][2]
@@ -175,6 +175,23 @@
         w_on(t, 8, 2, 0, to_twin)
         w_wait(t, 6, 2, False, 1)
         w_on(t, 9, 2, 1, to_twin)
+
+    def wo_rows(core, block):
+        return pl.ds(pl.multiple_of(block * COLS + core * HALF_ROWS, HALF_ROWS), HALF_ROWS)
+
+    core = seq % 2
+
+    def wo_from_partner():
+        send(wo_hbm.at[wo_rows(core, 0)], wo.at[wo_rows(core, 1)], w_send.at[2, 0], w_recv.at[2, 0], to_w)
+
+    def wo_to_twin():
+        ref = wo.at[wo_rows(core, 1)]
+        remote(ref, ref, w_send.at[2, 0], w_recv.at[2, 0], to_w).wait_recv()
+        send(ref, ref, w_send.at[2, 1], w_recv.at[2, 1], to_twin)
+
+    def wo_finish():
+        ref = wo.at[wo_rows(1 - core, 1)]
+        remote(ref, ref, w_send.at[2, 1], w_recv.at[2, 1], to_w).wait_recv()
 
     def w_finish(t):
         w_wait(t, 3, 0, True, None)
@@ -259,10 +276,10 @@
     scale_block(k_n)
     ag_wait(3, k_o, h1)
     scale_block(k_o)
-    w_stage1(1)
-    w_from_partner(2)
     w_stage2(0)
     w_stage3(0)
+    w_stage1(1)
+    wo_from_partner()
     ag_wait(4, k_d, h1)
     ag_wait(5, k_d, h2)
     scale_block(k_d)
@@ -298,8 +315,6 @@
     lax.fori_loop(0, 2, project_control, 0)
     v_copy.wait()
     project_values(0)
-    w_stage2(1)
-    w_stage1(2)
 
     def compact(c, carry_):
         rows = pl.ds(pl.multiple_of(c * CHUNK, CHUNK), CHUNK)
@@ -374,14 +389,9 @@
 
         lax.fori_loop(0, CHUNKS, states, 0)
 
-    states_of(0)
-    w_stage3(1)
-    w_finish(0)
-    project_values(1)
-    states_of(1)
-
     spread_of = [spread[:, 0:COLS], spread[:, COLS:]]
-    for blk in range(2):
+
+    def leave(blk):
         for c in range(CHUNKS):
             totx[blk, c] = jnp.exp2(exact(tot_sc[c], spread_of[blk]))
         f = chunk_state[blk * CHUNKS, :, 0:COLS]
@@ -396,22 +406,31 @@
             b = chunk_state[blk * CHUNKS + c, :, COLS:] + (
                 totx[blk, c, 0:1, :] * keep_b(begin, begin + CHUNK - 1)
             ) * b
-        st_send[:, blk] = jnp.concatenate(
+        st_send[blk] = jnp.concatenate(
             [f.reshape(NSEQ, GROUP, COLS), b.reshape(NSEQ, GROUP, COLS)], axis=1
         ).astype(BF16)
 
-    def state_copy(k):
+        def send_state(k, carry_):
+            state_copy(blk, k).start()
+            return carry_
+
+        lax.fori_loop(1, NSEQ, send_state, 0)
+        st_recv[blk, seq] = st_send[blk, seq]
+
+    def state_copy(blk, k):
         peer = (seq + k) % NSEQ
         return remote(
-            st_send.at[peer], st_recv.at[seq], s1_send.at[k], s1_recv.at[k], {"seq": peer}
+            st_send.at[blk, peer], st_recv.at[blk, seq], s1_send.at[blk, k], s1_recv.at[blk, k], {"seq": peer}
         )
 
-    def send_state(k, carry_):
-        state_copy(k).start()
-        return carry_
-
-    lax.fori_loop(1, NSEQ, send_state, 0)
-    st_recv[seq] = st_send[seq]
+    states_of(0)
+    leave(0)
+    w_finish(0)
+    project_values(1)
+    w_stage2(1)
+    states_of(1)
+    leave(1)
+    w_stage3(1)
 
     left = iota((CHUNK, 128), 1) < HEAD_DIM
 
@@ -448,9 +467,6 @@
 
         lax.fori_loop(0, CHUNKS, within, 0)
 
-    within_of(0)
-    w_stage2(2)
-
     def await_log(k, carry_):
         src = (seq + NSEQ - k) % NSEQ
         remote(
@@ -458,19 +474,15 @@
         ).wait_recv()
         return carry_
 
-    lax.fori_loop(1, NSEQ, await_log, 0)
-    keep_x[...] = jnp.exp2(exact(log_recv[...].reshape(NSEQ * 8, 128), spread)).reshape(NSEQ, 8, 2 * COLS)
-
-    def await_state(k, carry_):
-        src = (seq + NSEQ - k) % NSEQ
-        remote(
-            st_send.at[src], st_recv.at[src], s1_send.at[k], s1_recv.at[k], {"seq": src}
-        ).wait_recv()
-        return carry_
-
-    lax.fori_loop(1, NSEQ, await_state, 0)
-
-    for blk in range(2):
+    def scan_devices(blk):
+        def await_state(k, carry_):
+            src = (seq + NSEQ - k) % NSEQ
+            remote(
+                st_send.at[blk, src], st_recv.at[blk, src], s1_send.at[blk, k], s1_recv.at[blk, k], {"seq": src}
+            ).wait_recv()
+            return carry_
+
+        lax.fori_loop(1, NSEQ, await_state, 0)
         lanes = slice(blk * COLS, (blk + 1) * COLS)
         now = jnp.zeros((GROUP, COLS), F32)
         for d in range(NSEQ):
@@ -478,47 +490,50 @@
             if d < NSEQ - 1:
                 begin = d * ROWS
                 kept = keep_x[d, :, lanes] * keep_f(begin, begin + ROWS - 1)
-                now = st_recv[d, blk].astype(F32)[0:GROUP] + kept * now
+                now = st_recv[blk, d].astype(F32)[0:GROUP] + kept * now
         now = jnp.zeros((GROUP, COLS), F32)
         for d in range(NSEQ - 1, -1, -1):
-            en_send[d, blk] = jnp.concatenate([enter[d, blk], now], axis=0).astype(BF16)
+            en_send[blk, d] = jnp.concatenate([enter[d, blk], now], axis=0).astype(BF16)
             if d > 0:
                 begin = d * ROWS
                 kept = keep_x[d, :, lanes] * keep_b(begin, begin + ROWS - 1)
-                now = st_recv[d, blk].astype(F32)[GROUP : 2 * GROUP] + kept * now
-
-    def enter_copy(k):
+                now = st_recv[blk, d].astype(F32)[GROUP : 2 * GROUP] + kept * now
+
+        def send_enter(k, carry_):
+            enter_copy(blk, k).start()
+            return carry_
+
+        lax.fori_loop(1, NSEQ, send_enter, 0)
+        en_recv[blk, seq] = en_send[blk, seq]
+
+    def enter_copy(blk, k):
         peer = (seq + k) % NSEQ
         return remote(
-            en_send.at[peer], en_recv.at[seq], s2_send.at[k], s2_recv.at[k], {"seq": peer}
+            en_send.at[blk, peer], en_recv.at[blk, seq], s2_send.at[blk, k], s2_recv.at[blk, k], {"seq": peer}
         )
 
-    def send_enter(k, carry_):
-        enter_copy(k).start()
-        return carry_
-
-    lax.fori_loop(1, NSEQ, send_enter, 0)
-    en_recv[seq] = en_send[seq]
-    w_stage3(2)
-
+    lax.fori_loop(1, NSEQ, await_log, 0)
+    keep_x[...] = jnp.exp2(exact(log_recv[...].reshape(NSEQ * 8, 128), spread)).reshape(NSEQ, 8, 2 * COLS)
+    scan_devices(0)
+    within_of(0)
+    scan_devices(1)
+    wo_to_twin()
     within_of(1)
-
     g_copy.wait()
     project_gates(0)
     w_finish(1)
     project_gates(1)
 
-    def await_enter(k, carry_):
-        src = (seq + NSEQ - k) % NSEQ
-        remote(
-            en_send.at[src], en_recv.at[src], s2_send.at[k], s2_recv.at[k], {"seq": src}
-        ).wait_recv()
-        return carry_
-
-    lax.fori_loop(1, NSEQ, await_enter, 0)
-
-    for blk in range(2):
-        both = en_recv[:, blk].astype(F32)
+    def outside(blk):
+        def await_enter(k, carry_):
+            src = (seq + NSEQ - k) % NSEQ
+            remote(
+                en_send.at[blk, src], en_recv.at[blk, src], s2_send.at[blk, k], s2_recv.at[blk, k], {"seq": src}
+            ).wait_recv()
+            return carry_
+
+        lax.fori_loop(1, NSEQ, await_enter, 0)
+        both = en_recv[blk].astype(F32)
         f = both[:, 0:GROUP].reshape(STATE, COLS)
         b = both[:, GROUP : 2 * GROUP].reshape(STATE, COLS)
         for c in range(CHUNKS):
@@ -540,6 +555,9 @@
                     totx[blk, c, 0:1, :] * keep_b(begin, begin + CHUNK - 1)
                 ) * b
 
+    outside(0)
+    outside(1)
+
     ones = jnp.ones((8, COLS), BF16)
     row8 = iota((8, CHUNK), 0)
 
@@ -555,91 +573,104 @@
                 hi = sq.astype(BF16)
                 lo = (sq - hi.astype(F32)).astype(BF16)
                 sums = sums + jnp.where(row8 == d, dot_nt(ones, hi) + dot_nt(ones, lo), 0.0)
-        ps_mine[:, rows] = sums
+        ps_mine[c // 2, :, pl.ds(pl.multiple_of((c % 2) * CHUNK, CHUNK), CHUNK)] = sums
         return carry_
 
-    lax.fori_loop(0, CHUNKS, gate, 0)
-    for k, device in enumerate((to_d, to_n, to_o)):
-        send(ps_mine, ps_buf.at[k], ps_send.at[k], ps_recv.at[k], device)
-    w_finish(2)
+    def send_sums(half):
+        for k, device in enumerate((to_d, to_n, to_o)):
+            send(ps_mine.at[half], ps_buf.at[half, k], ps_send.at[half, k], ps_recv.at[half, k], device)
+
+    def norm_half(half):
+        for k in range(3):
+            remote(
+                ps_mine.at[half], ps_buf.at[half, k], ps_send.at[half, k], ps_recv.at[half, k], to_n
+            ).wait_recv()
+        sums = ps_mine[half] + ps_buf[half, 0] + ps_buf[half, 1] + ps_buf[half, 2]
+        scale = lax.rsqrt(sums * (1.0 / (COLS * NCHAN)) + norm_eps)
+        scale = jnp.concatenate([scale, jnp.zeros((CHUNK - 8, HALF_ROWS), F32)], axis=0)
+        for i in range(2):
+            c = 2 * half + i
+            rows = slice(c * CHUNK, (c + 1) * CHUNK)
+            r = scale[:, i * CHUNK : (i + 1) * CHUNK].T
+            for blk in range(2):
+                both = y_f[blk, rows, :] * r[:, 0:1] + y_b[blk, rows, :] * r[:, 1:2]
+                comb[rows, blk * COLS : (blk + 1) * COLS] = (both * gg[blk]).astype(BF16)
+
+    lax.fori_loop(0, 2, gate, 0)
+    send_sums(0)
+    lax.fori_loop(2, 4, gate, 0)
+    send_sums(1)
+    wo_finish()
     o_copy.wait()
     remote(ggain_ref, gg.at[1], ag_send.at[6], ag_recv.at[6], to_w).wait_recv()
-    for k in range(3):
-        remote(ps_mine, ps_buf.at[k], ps_send.at[k], ps_recv.at[k], to_n).wait_recv()
-    sums = ps_mine[...] + ps_buf[0] + ps_buf[1] + ps_buf[2]
-    scale = lax.rsqrt(sums * (1.0 / (COLS * NCHAN)) + norm_eps)
-    scale = jnp.concatenate([scale, jnp.zeros((CHUNK - 8, ROWS), F32)], axis=0)
-    for c in range(CHUNKS):
-        rinv[c * CHUNK : (c + 1) * CHUNK, :] = scale[:, c * CHUNK : (c + 1) * CHUNK].T
-
-    def combine(c, carry_):
-        rows = pl.ds(pl.multiple_of(c * CHUNK, CHUNK), CHUNK)
-        r = rinv[rows, :]
-        for blk in range(2):
-            both = y_f[blk, rows, :] * r[:, 0:1] + y_b[blk, rows, :] * r[:, 1:2]
-            comb[rows, blk * COLS : (blk + 1) * COLS] = (both * gg[blk]).astype(BF16)
-        return carry_
-
-    lax.fori_loop(0, CHUNKS, combine, 0)
-
-    def out_block(k):
+
+    def out_block(k, half):
         lanes = pl.ds(pl.multiple_of(k * COLS, COLS), COLS)
-
-        def block(i, carry_):
-            rows = pl.ds(pl.multiple_of(i * 256, 256), 256)
-            part[k, rows, :] = (
-                dot(comb[rows, 0:COLS], wo[0, :, lanes]) + dot(comb[rows, COLS:], wo[1, :, lanes])
-            ).astype(BF16)
-            return carry_
-
-        lax.fori_loop(0, 2, block, 0)
-
-    def rs(kind, src, dst, device):
-        send(src, dst, rs_send.at[kind], rs_recv.at[kind], device)
-
-    def rs_wait(kind, dst):
-        remote(part.at[k_me, h1], dst, rs_send.at[kind], rs_recv.at[kind], to_n).wait_recv()
+        rows = pl.ds(half * HALF_ROWS, HALF_ROWS)
+        part[k, rows, :] = dot(comb[rows, :], wo[:, lanes]).astype(BF16)
+
+    def quarter(half, i):
+        return pl.ds((2 * half + i) * CHUNK, CHUNK)
+
+    def rs(half, kind, src, dst, device):
+        send(src, dst, rs_send.at[half, kind], rs_recv.at[half, kind], device)
+
+    def rs_wait(half, kind, dst):
+        remote(
+            part.at[k_me, quarter(0, 0)], dst, rs_send.at[half, kind], rs_recv.at[half, kind], to_n
+        ).wait_recv()
 
     def add(block, rows, ref):
         part[block, rows, :] = (part[block, rows, :].astype(F32) + ref[...].astype(F32)).astype(BF16)
 
-    out_block(k_d)
-    rs(0, part.at[k_d, h1], relay.at[0], to_o)
-    rs(1, part.at[k_d, h2], relay.at[1], to_n)
-
-    def out_second(i, carry_):
-        out_block(jnp.where(i == 0, k_n, k_o))
-        return carry_
-
-    lax.fori_loop(0, 2, out_second, 0)
-    rs(2, part.at[k_n, h2], rs_buf.at[0, h2], to_n)
-    rs(4, part.at[k_o, h1], rs_buf.at[1, h1], to_o)
-    out_block(k_me)
-    rs_wait(0, relay.at[0])
-    add(k_n, h1, relay.at[0])
-    rs(3, part.at[k_n, h1], rs_buf.at[0, h1], to_n)
-    rs_wait(1, relay.at[1])
-    add(k_o, h2, relay.at[1])
-    rs(5, part.at[k_o, h2], rs_buf.at[1, h2], to_o)
-
-    def finish(i, rows):
+    def produce(half):
+        q1, q2 = quarter(half, 0), quarter(half, 1)
+        out_block(k_d, half)
+        rs(half, 0, part.at[k_d, q1], relay.at[half, 0], to_o)
+        rs(half, 1, part.at[k_d, q2], relay.at[half, 1], to_n)
+        out_block(k_n, half)
+        rs(half, 2, part.at[k_n, q2], rs_buf.at[0, q2], to_n)
+        out_block(k_o, half)
+        rs(half, 4, part.at[k_o, q1], rs_buf.at[1, q1], to_o)
+
+    def hand_on(half):
+        q1, q2 = quarter(half, 0), quarter(half, 1)
+        rs_wait(half, 0, relay.at[half, 0])
+        add(k_n, q1, relay.at[half, 0])
+        rs(half, 3, part.at[k_n, q1], rs_buf.at[0, q1], to_n)
+        rs_wait(half, 1, relay.at[half, 1])
+        add(k_o, q2, relay.at[half, 1])
+        rs(half, 5, part.at[k_o, q2], rs_buf.at[1, q2], to_o)
+
+    def finish(half):
+        q1, q2 = quarter(half, 0), quarter(half, 1)
+        rs_wait(half, 4, rs_buf.at[1, q1])
+        rs_wait(half, 2, rs_buf.at[0, q2])
+        rs_wait(half, 3, rs_buf.at[0, q1])
+        rs_wait(half, 5, rs_buf.at[1, q2])
+        rows = pl.ds(half * HALF_ROWS, HALF_ROWS)
         total = part[k_me, rows, :].astype(F32) + rs_buf[0, rows, :].astype(F32) + rs_buf[1, rows, :].astype(F32)
         out_ref[rows, :] = dot(total.astype(BF16), flip).astype(BF16)
 
-    rs_wait(4, rs_buf.at[1, h1])
-    rs_wait(2, rs_buf.at[0, h2])
-    rs_wait(3, rs_buf.at[0, h1])
-    finish(0, h1)
-    rs_wait(5, rs_buf.at[1, h2])
-    finish(1, h2)
+    norm_half(0)
+    produce(0)
+    norm_half(1)
+    hand_on(0)
+    produce(1)
+    out_block(k_me, 0)
+    out_block(k_me, 1)
+    hand_on(1)
+    finish(0)
+    finish(1)
 
     for copy in started:
         copy.wait_send()
 
     def sent_seq(k, carry_):
         log_copy(k).wait_send()
-        state_copy(k).wait_send()
-        enter_copy(k).wait_send()
+        for blk in range(2):
+            state_copy(blk, k).wait_send()
+            enter_copy(blk, k).wait_send()
         return carry_
 
     lax.fori_loop(1, NSEQ, sent_seq, 0)
@@ -657,7 +688,7 @@
         pltpu.VMEM((2, HALF, COLS), BF16),
         pltpu.VMEM((2, HALF, COLS), BF16),
         pltpu.VMEM((CTRL, HALF), BF16),
-        pltpu.VMEM((2, COLS, HALF), BF16),
+        pltpu.VMEM((2 * COLS, HALF), BF16),
         pltpu.VMEM((2, 1, COLS), F32),
         pltpu.VMEM((4, ROWS, COLS), BF16),
         pltpu.VMEM((ROWS, HALF), BF16),
@@ -679,19 +710,19 @@
         pltpu.VMEM((2, CHUNKS, 8, COLS), F32),
         pltpu.VMEM((NSEQ, 8, 128), F32),
         pltpu.VMEM((NSEQ, 8, 2 * COLS), F32),
-        pltpu.VMEM((NSEQ, 2, 2 * GROUP, COLS), BF16),
-        pltpu.VMEM((NSEQ, 2, 2 * GROUP, COLS), BF16),
+        pltpu.VMEM((2, NSEQ, 2 * GROUP, COLS), BF16),
+        pltpu.VMEM((2, NSEQ, 2 * GROUP, COLS), BF16),
         pltpu.VMEM((NSEQ, 2, GROUP, COLS), F32),
-        pltpu.VMEM((NSEQ, 2, 2 * GROUP, COLS), BF16),
-        pltpu.VMEM((NSEQ, 2, 2 * GROUP, COLS), BF16),
+        pltpu.VMEM((2, NSEQ, 2 * GROUP, COLS), BF16),
+        pltpu.VMEM((2, NSEQ, 2 * GROUP, COLS), BF16),
         pltpu.VMEM((2, ROWS, COLS), F32),
         pltpu.VMEM((2, ROWS, COLS), F32),
-        pltpu.VMEM((3, 8, ROWS), F32),
-        pltpu.VMEM((8, ROWS), F32),
+        pltpu.VMEM((2, 3, 8, HALF_ROWS), F32),
+        pltpu.VMEM((2, 8, HALF_ROWS), F32),
         pltpu.VMEM((ROWS, 2 * COLS), BF16),
         pltpu.VMEM((4, ROWS, COLS), BF16),
         pltpu.VMEM((2, ROWS, COLS), BF16),
-        pltpu.VMEM((2, HALF_ROWS, COLS), BF16),
+        pltpu.VMEM((2, 2, CHUNK, COLS), BF16),
         dma((5,)),
         dma((7,)),
         dma((7,)),
@@ -699,14 +730,14 @@
         dma((3, 10)),
         dma((NSEQ,)),
         dma((NSEQ,)),
-        dma((NSEQ,)),
-        dma((NSEQ,)),
-        dma((NSEQ,)),
-        dma((NSEQ,)),
-        dma((3,)),
-        dma((3,)),
-        dma((6,)),
-        dma((6,)),
+        dma((2, NSEQ)),
+        dma((2, NSEQ)),
+        dma((2, NSEQ)),
+        dma((2, NSEQ)),
+        dma((2, 3)),
+        dma((2, 3)),
+        dma((2, 6)),
+        dma((2, 6)),
     ]
     return pl.pallas_call(
         kernel,

time: 95.3 us -> 85.3 us (0.90)
  Pallas kernels: 93.2 us -> 83.1 us
    pallas_call x1, Pallas kernels: 93.2 us -> 83.1 us  [local(): pl.pallas_call(kernel, name='mixer', out_shape=jax.ShapeDtypeStruct((ROWS...]
where the time goes in v1:
time: 85.3 us; the launch traced here: 85 us
  Pallas kernels  83.1 us (97%)
  local copies, waits for them, and re-layouts  1.87 us (2%)
    pallas_call x1, Pallas kernels, local(): pl.pallas_call(kernel, name='mixer', out_shape=jax.ShapeDtypeStruct((ROWS...  83.1 us
    unnamed x1, local copies, waits for them, and re-layouts  1.87 us

profile of v1, /device:TPU:0, one launch (start us, length us, event | category | flops | bytes accessed | tf_op | source)
XLA Modules:
  0.0 85.0 jit_solution(2215465043614060304)
XLA Ops:
  0.0 83.1 %mixer.1 = bf16[512,512]{1,0:T(8,128)(2,1)} custom-call(bf16[512,512]{1,0:T(8,128)(2,1)} %x_hbm.1, f32[4,1,512]{2,1,0:T(1,128)} %bitcast.7, bf16[2048,512]{1,0:T(8,128)(2,1)} %wv_hbm.1, bf16[2048,512]{1,0:T(8,128)(2,1)} %wg_hbm.1, bf16[320,2048]{1,0:T(8,128)(2,1)} %bitcast.6, f32[1,64]{1,0:T(1,128)} %bitcast.9, f32[1,64]{1,0:T(1,128)} %bitcast.10, ...), custom_call_target="tpu_custom_call" | custom-call | tf_op jit(solution)/shard_map/mixer/pallas_call | solution.py:742
  83.1 1.9 %copy.13 = bf16[512,512]{1,0:T(8,128)(2,1)} copy(bf16[512,512]{1,0:T(8,128)(2,1)} %mixer.1) | data formatting | bytes 1048576

commit v2 on v1

--- a/solution.py
+++ b/solution.py
@@ -65,9 +65,9 @@
     out_ref,
     x_v, wv, wg, wc, wo, gg, gath, xg, sumsq, rinv,
     c_sc, factors, scores_sc, l_sc, e_sc, lt_sc, et_sc, wval, val, act, reach, chunk_state, tot_sc, totx,
-    log_recv, keep_x, st_send, st_recv, enter, en_send, en_recv, y_f, y_b,
+    log_recv, keep_x, st_send, st_recv, enter, en_send, en_recv, inner, y_f, y_b,
     ps_buf, ps_mine, comb, part, rs_buf, relay,
-    loc_sem, ag_send, ag_recv, w_send, w_recv, s0_send, s0_recv, s1_send, s1_recv, s2_send, s2_recv,
+    loc_sem, word, ag_send, ag_recv, w_send, w_recv, s0_send, s0_recv, s1_send, s1_recv, s2_send, s2_recv,
     ps_send, ps_recv, rs_send, rs_recv,
 ):
     seq = lax.axis_index("seq")
@@ -95,11 +95,17 @@
     for device in (to_n, to_o, to_d, to_w):
         pl.semaphore_signal(barrier, inc=1, device_id=device, device_id_type=MESH)
 
-    def greet_seq(k, carry_):
-        pl.semaphore_signal(barrier, inc=1, device_id={"seq": (seq + k) % NSEQ}, device_id_type=MESH)
-        return carry_
-
-    lax.fori_loop(1, NSEQ, greet_seq, 0)
+    to_across = {"seq": seq + 2 - 4 * ((seq // 2) % 2)}
+    near = (to_right, to_left, to_twin, to_across)
+    for device in near:
+        pl.semaphore_signal(barrier, inc=1, device_id=device, device_id_type=MESH)
+
+    def spread_word(i):
+        for device in near:
+            pl.semaphore_signal(word.at[i], inc=1, device_id=device, device_id_type=MESH)
+
+    def hear(i):
+        pl.semaphore_wait(word.at[i], 4)
 
     x_copy = pltpu.make_async_copy(x_hbm, x_v, loc_sem.at[0])
     x_copy.start()
@@ -115,10 +121,8 @@
     gath[k_me] = dot(x_v[...], flip).astype(BF16)
     gg[0] = ggain_ref[...]
 
-    pl.semaphore_wait(barrier, 4 + NSEQ - 1)
-
-    h1, h2 = pl.ds(0, HALF_ROWS), pl.ds(HALF_ROWS, HALF_ROWS)
-    whole = pl.ds(0, ROWS)
+    pl.semaphore_wait(barrier, 8)
+
     started = []
 
     def send(src, dst, send_sem, recv_sem, device):
@@ -126,13 +130,13 @@
         copy.start()
         started.append(copy)
 
-    def ag(kind, block, rows, device):
-        ref = gath.at[block, rows]
-        send(ref, ref, ag_send.at[kind], ag_recv.at[kind], device)
-
-    def ag_wait(kind, block, rows):
-        ref = gath.at[block, rows]
-        remote(ref, ref, ag_send.at[kind], ag_recv.at[kind], to_n).wait_recv()
+    def ag(half, kind, block, q, device):
+        ref = gath.at[block, pl.ds((2 * half + q) * CHUNK, CHUNK)]
+        send(ref, ref, ag_send.at[half, kind], ag_recv.at[half, kind], device)
+
+    def ag_wait(half, kind, block, q):
+        ref = gath.at[block, pl.ds((2 * half + q) * CHUNK, CHUNK)]
+        remote(ref, ref, ag_send.at[half, kind], ag_recv.at[half, kind], to_n).wait_recv()
 
     tensors = ((wv_hbm, wv, HALF // 8), (wg_hbm, wg, HALF // 8))
 
@@ -200,17 +204,38 @@
         w_wait(t, 8, 2, True, 0)
         w_wait(t, 9, 2, True, 1)
 
-    ag(0, k_me, h1, to_n)
-    ag(2, k_me, h2, to_o)
+    def ag_own(half):
+        ag(half, 0, k_me, 0, to_n)
+        ag(half, 2, k_me, 1, to_o)
+        ag(half, 1, k_me, 1, to_n)
+        ag(half, 3, k_me, 0, to_o)
+
+    def ag_relay(half):
+        ag_wait(half, 0, k_n, 0)
+        ag(half, 4, k_n, 0, to_o)
+        ag_wait(half, 2, k_o, 1)
+        ag(half, 5, k_o, 1, to_n)
+
+    def ag_near(half):
+        ag_wait(half, 1, k_n, 1)
+        scale_block(k_n, half)
+        ag_wait(half, 3, k_o, 0)
+        scale_block(k_o, half)
+
+    def ag_far(half):
+        ag_wait(half, 4, k_d, 0)
+        ag_wait(half, 5, k_d, 1)
+        scale_block(k_d, half)
+
+    ag_own(0)
     w_from_partner(0)
-    ag(1, k_me, h2, to_n)
-    ag(3, k_me, h1, to_o)
+    spread_word(0)
     w_from_partner(1)
-    send(ggain_ref, gg.at[1], ag_send.at[6], ag_recv.at[6], to_w)
+    send(ggain_ref, gg.at[1], ag_send.at[0, 6], ag_recv.at[0, 6], to_w)
     for copy in (v_copy, c_copy, g_copy, o_copy):
         copy.start()
 
-    def scale_block(k):
+    def scale_block(k, half):
         gain = gain_ref[k]
         lanes = pl.ds(pl.multiple_of(k * COLS, COLS), COLS)
 
@@ -222,10 +247,10 @@
             sumsq[rows, :] += sq[:, 0:128] + sq[:, 128:256] + sq[:, 256:384] + sq[:, 384:512]
             return carry_
 
-        lax.fori_loop(0, ROWS // 64, scale_rows, 0)
+        lax.fori_loop(4 * half, 4 * half + 4, scale_rows, 0)
 
     sumsq[...] = jnp.zeros_like(sumsq)
-    scale_block(k_me)
+    scale_block(k_me, 0)
 
     lane = iota((HEADS, 128), 1)
     head = iota((HEADS, 128), 0)
@@ -267,54 +292,28 @@
     lower = jnp.where(sub >= lan, 1.0, 0.0).astype(BF16)
     upper = jnp.where(sub <= lan, 1.0, 0.0).astype(BF16)
 
-    ag_wait(0, k_n, h1)
-    ag(4, k_n, h1, to_o)
-    ag_wait(2, k_o, h2)
-    ag(5, k_o, h2, to_n)
-    w_stage1(0)
-    ag_wait(1, k_n, h2)
-    scale_block(k_n)
-    ag_wait(3, k_o, h1)
-    scale_block(k_o)
-    w_stage2(0)
-    w_stage3(0)
-    w_stage1(1)
-    wo_from_partner()
-    ag_wait(4, k_d, h1)
-    ag_wait(5, k_d, h2)
-    scale_block(k_d)
-
-    for i in range(CHUNKS):
-        rows = pl.ds(i * CHUNK, CHUNK)
-        total = jnp.sum(sumsq[rows, :], axis=1, keepdims=True)
-        rinv[rows, :] = jnp.broadcast_to(lax.rsqrt(total * (1.0 / HALF) + norm_eps), (CHUNK, 128))
-
-    def project_control(i, carry_):
-        rows = pl.ds(pl.multiple_of(i * 256, 256), 256)
+    def row_scale(half):
+        for i in range(2 * half, 2 * half + 2):
+            rows = pl.ds(i * CHUNK, CHUNK)
+            total = jnp.sum(sumsq[rows, :], axis=1, keepdims=True)
+            rinv[rows, :] = jnp.broadcast_to(lax.rsqrt(total * (1.0 / HALF) + norm_eps), (CHUNK, 128))
+
+    def project_control(half):
+        rows = pl.ds(half * HALF_ROWS, HALF_ROWS)
         c_sc[rows, :] = (dot_nt(xg[rows, :], wc[...]) * rinv[rows, :][:, 0:1]).astype(BF16)
-        return carry_
-
-    def project_values(blk):
-        def go(i, carry_):
-            rows = pl.ds(pl.multiple_of(i * 256, 256), 256)
-            val[blk, rows, :] = (dot(xg[rows, :], wv[blk]) * rinv[rows, :][:, 0:1]).astype(BF16)
-            return carry_
-
-        lax.fori_loop(0, 2, go, 0)
+
+    def project_values(blk, half):
+        rows = pl.ds(half * HALF_ROWS, HALF_ROWS)
+        val[blk, rows, :] = (dot(xg[rows, :], wv[blk]) * rinv[rows, :][:, 0:1]).astype(BF16)
 
     def project_gates(blk):
         def go(i, carry_):
-            rows = pl.ds(pl.multiple_of(i * 256, 256), 256)
+            rows = pl.ds(pl.multiple_of(i * HALF_ROWS, HALF_ROWS), HALF_ROWS)
             g = (dot(xg[rows, :], wg[blk]) * rinv[rows, :][:, 0:1]).astype(BF16).astype(F32)
             act[blk, rows, :] = g / (1.0 + jnp.exp(-g))
             return carry_
 
         lax.fori_loop(0, 2, go, 0)
-
-    c_copy.wait()
-    lax.fori_loop(0, 2, project_control, 0)
-    v_copy.wait()
-    project_values(0)
 
     def compact(c, carry_):
         rows = pl.ds(pl.multiple_of(c * CHUNK, CHUNK), CHUNK)
@@ -355,23 +354,7 @@
         scores_sc[c] = jnp.where(seg == seg_at(begin + lan), scores, 0.0)
         return carry_
 
-    lax.fori_loop(0, CHUNKS, compact, 0)
-    tot_sc[CHUNKS] = tot_sc[0] + tot_sc[1] + tot_sc[2] + tot_sc[3]
-    log_recv[seq] = tot_sc[CHUNKS]
-
-    def log_copy(k):
-        peer = (seq + k) % NSEQ
-        return remote(
-            tot_sc.at[CHUNKS], log_recv.at[seq], s0_send.at[k], s0_recv.at[k], {"seq": peer}
-        )
-
-    def send_log(k, carry_):
-        log_copy(k).start()
-        return carry_
-
-    lax.fori_loop(1, NSEQ, send_log, 0)
-
-    def states_of(blk):
+    def states_of(blk, first):
         spread_blk = spread_b[:, blk * COLS : (blk + 1) * COLS]
 
         def states(c, carry_):
@@ -387,7 +370,7 @@
             chunk_state[blk * CHUNKS + c] = dot_tn(c_sc[rows, 0:STATE], weighted)
             return carry_
 
-        lax.fori_loop(0, CHUNKS, states, 0)
+        lax.fori_loop(first, first + 2, states, 0)
 
     spread_of = [spread[:, 0:COLS], spread[:, COLS:]]
 
@@ -423,18 +406,9 @@
             st_send.at[blk, peer], st_recv.at[blk, seq], s1_send.at[blk, k], s1_recv.at[blk, k], {"seq": peer}
         )
 
-    states_of(0)
-    leave(0)
-    w_finish(0)
-    project_values(1)
-    w_stage2(1)
-    states_of(1)
-    leave(1)
-    w_stage3(1)
-
     left = iota((CHUNK, 128), 1) < HEAD_DIM
 
-    def within_of(blk):
+    def within_of(blk, first):
         def within(c, carry_):
             rows = pl.ds(pl.multiple_of(c * CHUNK, CHUNK), CHUNK)
             scores = scores_sc[c]
@@ -465,7 +439,64 @@
                 y_b[blk, rows, lanes] = y[CHUNK:] + direct
             return carry_
 
-        lax.fori_loop(0, CHUNKS, within, 0)
+        lax.fori_loop(first, first + 2, within, 0)
+
+    ag_relay(0)
+    ag_own(1)
+    hear(0)
+    spread_word(1)
+    scale_block(k_me, 1)
+    ag_near(0)
+    w_stage1(0)
+    hear(1)
+    spread_word(2)
+    ag_far(0)
+    row_scale(0)
+    c_copy.wait()
+    project_control(0)
+    v_copy.wait()
+    project_values(0, 0)
+    ag_relay(1)
+    lax.fori_loop(0, 2, compact, 0)
+    w_stage2(0)
+    w_stage1(1)
+    wo_from_partner()
+    states_of(0, 0)
+    within_of(0, 0)
+    w_stage3(0)
+
+    ag_near(1)
+    ag_far(1)
+    row_scale(1)
+    project_control(1)
+    project_values(0, 1)
+    lax.fori_loop(2, 4, compact, 0)
+    hear(2)
+    tot_sc[CHUNKS] = tot_sc[0] + tot_sc[1] + tot_sc[2] + tot_sc[3]
+    log_recv[seq] = tot_sc[CHUNKS]
+
+    def log_copy(k):
+        peer = (seq + k) % NSEQ
+        return remote(
+            tot_sc.at[CHUNKS], log_recv.at[seq], s0_send.at[k], s0_recv.at[k], {"seq": peer}
+        )
+
+    def send_log(k, carry_):
+        log_copy(k).start()
+        return carry_
+
+    lax.fori_loop(1, NSEQ, send_log, 0)
+
+    states_of(0, 2)
+    w_stage2(1)
+    leave(0)
+    w_finish(0)
+    project_values(1, 0)
+    project_values(1, 1)
+    states_of(1, 0)
+    w_stage3(1)
+    states_of(1, 2)
+    leave(1)
 
     def await_log(k, carry_):
         src = (seq + NSEQ - k) % NSEQ
@@ -515,12 +546,13 @@
     lax.fori_loop(1, NSEQ, await_log, 0)
     keep_x[...] = jnp.exp2(exact(log_recv[...].reshape(NSEQ * 8, 128), spread)).reshape(NSEQ, 8, 2 * COLS)
     scan_devices(0)
-    within_of(0)
+    within_of(0, 2)
+    g_copy.wait()
+    project_gates(0)
     scan_devices(1)
     wo_to_twin()
-    within_of(1)
-    g_copy.wait()
-    project_gates(0)
+    within_of(1, 0)
+    within_of(1, 2)
     w_finish(1)
     project_gates(1)
 
@@ -537,19 +569,15 @@
         f = both[:, 0:GROUP].reshape(STATE, COLS)
         b = both[:, GROUP : 2 * GROUP].reshape(STATE, COLS)
         for c in range(CHUNKS):
-            rows = pl.ds(c * CHUNK, CHUNK)
             begin = base + c * CHUNK
-            cc = c_sc[rows, STATE : 2 * STATE]
-            y_f[blk, rows, :] += dot(cc, f.astype(BF16)) * reach[blk, 0, rows, :].astype(F32)
+            inner[blk, c, 0] = f.astype(BF16)
             if c < CHUNKS - 1:
                 f = chunk_state[blk * CHUNKS + c, :, 0:COLS] + (
                     totx[blk, c, 0:1, :] * keep_f(begin, begin + CHUNK - 1)
                 ) * f
         for c in range(CHUNKS - 1, -1, -1):
-            rows = pl.ds(c * CHUNK, CHUNK)
             begin = base + c * CHUNK
-            cc = c_sc[rows, STATE : 2 * STATE]
-            y_b[blk, rows, :] += dot(cc, b.astype(BF16)) * reach[blk, 1, rows, :].astype(F32)
+            inner[blk, c, 1] = b.astype(BF16)
             if c > 0:
                 b = chunk_state[blk * CHUNKS + c, :, COLS:] + (
                     totx[blk, c, 0:1, :] * keep_b(begin, begin + CHUNK - 1)
@@ -564,10 +592,12 @@
     def gate(c, carry_):
         rows = pl.ds(pl.multiple_of(c * CHUNK, CHUNK), CHUNK)
         sums = jnp.zeros((8, CHUNK), F32)
+        cc = c_sc[rows, STATE : 2 * STATE]
         for blk in range(2):
             a = act[blk, rows, :]
             for d, y in enumerate((y_f, y_b)):
-                v = y[blk, rows, :] * a
+                added = dot(cc, inner[blk, c, d]) * reach[blk, d, rows, :].astype(F32)
+                v = (y[blk, rows, :] + added) * a
                 y[blk, rows, :] = v
                 sq = v * v
                 hi = sq.astype(BF16)
@@ -602,7 +632,7 @@
     send_sums(1)
     wo_finish()
     o_copy.wait()
-    remote(ggain_ref, gg.at[1], ag_send.at[6], ag_recv.at[6], to_w).wait_recv()
+    remote(ggain_ref, gg.at[1], ag_send.at[0, 6], ag_recv.at[0, 6], to_w).wait_recv()
 
     def out_block(k, half):
         lanes = pl.ds(pl.multiple_of(k * COLS, COLS), COLS)
@@ -715,6 +745,7 @@
         pltpu.VMEM((NSEQ, 2, GROUP, COLS), F32),
         pltpu.VMEM((2, NSEQ, 2 * GROUP, COLS), BF16),
         pltpu.VMEM((2, NSEQ, 2 * GROUP, COLS), BF16),
+        pltpu.VMEM((2, CHUNKS, 2, STATE, COLS), BF16),
         pltpu.VMEM((2, ROWS, COLS), F32),
         pltpu.VMEM((2, ROWS, COLS), F32),
         pltpu.VMEM((2, 3, 8, HALF_ROWS), F32),
@@ -724,8 +755,9 @@
         pltpu.VMEM((2, ROWS, COLS), BF16),
         pltpu.VMEM((2, 2, CHUNK, COLS), BF16),
         dma((5,)),
-        dma((7,)),
-        dma((7,)),
+        pltpu.SemaphoreType.REGULAR((3,)),
+        dma((2, 7)),
+        dma((2, 7)),
         dma((3, 10)),
         dma((3, 10)),
         dma((NSEQ,)),

time: 85.3 us -> 83.3 us (0.977)
  Pallas kernels: 83.1 us -> 81.2 us
    pallas_call x1, Pallas kernels: 83.1 us -> 81.2 us  [local(): pl.pallas_call(kernel, name='mixer', out_shape=jax.ShapeDtypeStruct((ROWS...]
where the time goes in v2:
time: 83.3 us; the launch traced here: 83.1 us
  Pallas kernels  81.2 us (97%)
  local copies, waits for them, and re-layouts  1.87 us (2%)
    pallas_call x1, Pallas kernels, local(): pl.pallas_call(kernel, name='mixer', out_shape=jax.ShapeDtypeStruct((ROWS...  81.2 us
    unnamed x1, local copies, waits for them, and re-layouts  1.87 us

profile of v2, /device:TPU:0, one launch (start us, length us, event | category | flops | bytes accessed | tf_op | source)
XLA Modules:
  0.0 83.1 jit_solution(15709733679343769502)
XLA Ops:
  0.0 81.2 %mixer.1 = bf16[512,512]{1,0:T(8,128)(2,1)} custom-call(bf16[512,512]{1,0:T(8,128)(2,1)} %x_hbm.1, f32[4,1,512]{2,1,0:T(1,128)} %bitcast.7, bf16[2048,512]{1,0:T(8,128)(2,1)} %wv_hbm.1, bf16[2048,512]{1,0:T(8,128)(2,1)} %wg_hbm.1, bf16[320,2048]{1,0:T(8,128)(2,1)} %bitcast.6, f32[1,64]{1,0:T(1,128)} %bitcast.9, f32[1,64]{1,0:T(1,128)} %bitcast.10, ...), custom_call_target="tpu_custom_call" | custom-call | tf_op jit(solution)/shard_map/mixer/pallas_call | solution.py:774
  81.2 1.9 %copy.13 = bf16[512,512]{1,0:T(8,128)(2,1)} copy(bf16[512,512]{1,0:T(8,128)(2,1)} %mixer.1) | data formatting | bytes 1048576

commit v3 on v2

--- a/solution.py
+++ b/solution.py
@@ -488,13 +488,12 @@
     lax.fori_loop(1, NSEQ, send_log, 0)
 
     states_of(0, 2)
-    w_stage2(1)
     leave(0)
     w_finish(0)
     project_values(1, 0)
+    w_stage2(1)
     project_values(1, 1)
     states_of(1, 0)
-    w_stage3(1)
     states_of(1, 2)
     leave(1)
 
@@ -546,15 +545,16 @@
     lax.fori_loop(1, NSEQ, await_log, 0)
     keep_x[...] = jnp.exp2(exact(log_recv[...].reshape(NSEQ * 8, 128), spread)).reshape(NSEQ, 8, 2 * COLS)
     scan_devices(0)
+    w_stage3(1)
     within_of(0, 2)
     g_copy.wait()
     project_gates(0)
     scan_devices(1)
-    wo_to_twin()
     within_of(1, 0)
     within_of(1, 2)
     w_finish(1)
     project_gates(1)
+    wo_to_twin()
 
     def outside(blk):
         def await_enter(k, carry_):

time: 83.3 us -> 78.7 us (0.945)
  Pallas kernels: 81.2 us -> 76.6 us
    pallas_call x1, Pallas kernels: 81.2 us -> 76.6 us  [local(): pl.pallas_call(kernel, name='mixer', out_shape=jax.ShapeDtypeStruct((ROWS...]
where the time goes in v3:
time: 78.7 us; the launch traced here: 78.5 us
  Pallas kernels  76.6 us (97%)
  local copies, waits for them, and re-layouts  1.87 us (2%)
    pallas_call x1, Pallas kernels, local(): pl.pallas_call(kernel, name='mixer', out_shape=jax.ShapeDtypeStruct((ROWS...  76.6 us
    unnamed x1, local copies, waits for them, and re-layouts  1.87 us

profile of v3, /device:TPU:0, one launch (start us, length us, event | category | flops | bytes accessed | tf_op | source)
XLA Modules:
  0.0 78.5 jit_solution(15506654840986717771)
XLA Ops:
  0.0 76.6 %mixer.1 = bf16[512,512]{1,0:T(8,128)(2,1)} custom-call(bf16[512,512]{1,0:T(8,128)(2,1)} %x_hbm.1, f32[4,1,512]{2,1,0:T(1,128)} %bitcast.7, bf16[2048,512]{1,0:T(8,128)(2,1)} %wv_hbm.1, bf16[2048,512]{1,0:T(8,128)(2,1)} %wg_hbm.1, bf16[320,2048]{1,0:T(8,128)(2,1)} %bitcast.6, f32[1,64]{1,0:T(1,128)} %bitcast.9, f32[1,64]{1,0:T(1,128)} %bitcast.10, ...), custom_call_target="tpu_custom_call" | custom-call | tf_op jit(solution)/shard_map/mixer/pallas_call | solution.py:774
  76.6 1.9 %copy.13 = bf16[512,512]{1,0:T(8,128)(2,1)} copy(bf16[512,512]{1,0:T(8,128)(2,1)} %mixer.1) | data formatting | bytes 1048576
